TPU v7x, 32 devices: a whole 2x2x4 slice. The times are simulated.
32 devices in a mesh: gx: 8 (over y, x, core), gy: 4 (over z).
Axes of the slice: x: 2, y: 2, z: 4, core: 2. Of those that a mesh axis runs over, the one named last changes fastest.
Arguments:
- quotient_table: float32 [32768, 256], P(('gx', 'gy')), may hold values from -6 to 6
- quotient_acc: float32 [32768, 256], P(('gx', 'gy')), may hold values from 1 to 64
- remainder_table: float32 [4096, 256], replicated, may hold values from -6 to 6
- remainder_acc: float32 [4096, 256], P(('gx', 'gy')), may hold values from 1 to 64
- cotangent: bfloat16 [2048, 256], P(('gx', 'gy')), may hold values from -6 to 6
- quotient_ids: int32 [2048, 20], P(('gx', 'gy')), may hold values from 0 to 32767, as said below
- remainder_ids: int32 [2048, 20], P(('gx', 'gy')), may hold values from 0 to 4095
Outputs:
- new_quotient: float32 [32768, 256], P(('gx', 'gy'))
- new_quotient_acc: float32 [32768, 256], P(('gx', 'gy'))
- new_remainder: float32 [4096, 256], replicated
- new_remainder_acc: float32 [4096, 256], P(('gx', 'gy'))
Inputs may be any that keep to these rules, and one draw needn't show every extreme that they name: `quotient_ids`: call the rows k * 1024 to (k + 1) * 1024 - 1 the range of device k along gx+gy. Of the ids of one device's 64 samples, at most 80 fall in any one range; in every draw some range receives exactly 80 from every device.
All inputs are finite; a program needn't handle non-finite values.
Results may differ from a plain program's by a relative error of at most 0.0046.
Values may be sent and summed in bfloat16 or wider, within the bound.
A program may use at most 64 MiB of HBM per device.

v0:
```python
import jax
import jax.numpy as jnp
from jax import lax
from jax.sharding import PartitionSpec as P

LEARNING_RATE = 0.1
EPSILON = 1e-10


def adagrad(param, accum, grad):
    fresh = accum + grad * grad
    return (param - LEARNING_RATE * grad / (jnp.sqrt(fresh) + EPSILON), fresh)


def block_sums(ids, values, count):
    block = count
    if count > 1024 and count % 1024 == 0:
        block = 1024

    def one(first):
        wanted = first + jnp.arange(block, dtype=jnp.int32)
        hit = (wanted[:, None] == ids[None, :]).astype(jnp.bfloat16)
        return jnp.dot(hit, values, preferred_element_type=jnp.float32)

    firsts = jnp.arange(count // block, dtype=jnp.int32) * block
    return lax.map(one, firsts).reshape(count, values.shape[1])


def local(
    quotient_table,
    quotient_acc,
    remainder_table,
    remainder_acc,
    cotangent,
    quotient_ids,
    remainder_ids,
):
    devices = lax.axis_size(("gx", "gy"))
    q_dev, width = quotient_table.shape
    r_rows = remainder_table.shape[0]
    share = remainder_acc.shape[0]
    samples, bag = quotient_ids.shape
    count = samples * bag
    capacity = max(2, (2 * count + devices - 1) // devices)
    table_slots = devices * capacity
    flat_q = quotient_ids.reshape(count)
    flat_r = remainder_ids.reshape(count)
    owner = flat_q // q_dev
    local_row = flat_q - owner * q_dev
    order = jnp.argsort(owner, stable=True)
    sorted_owner = owner[order]
    column = jnp.arange(devices, dtype=jnp.int32)
    tally = jnp.sum((owner[:, None] == column[None, :]).astype(jnp.int32), axis=0)
    begins = jnp.cumsum(tally) - tally
    placed = sorted_owner * capacity + jnp.arange(count, dtype=jnp.int32) - begins[sorted_owner]
    target = jnp.zeros((count,), jnp.int32).at[order].set(placed)
    local_sent = (
        jnp.zeros((table_slots,), jnp.int32).at[target].set(local_row).reshape(devices, capacity)
    )
    cot_rows = jnp.repeat(cotangent, bag, axis=0)
    asked = lax.all_to_all(local_sent, ("gx", "gy"), split_axis=0, concat_axis=0, tiled=True)
    asked_flat = asked.reshape(table_slots)
    found = quotient_table[asked_flat].astype(jnp.bfloat16).reshape(devices, capacity, width)
    replies = lax.all_to_all(found, ("gx", "gy"), split_axis=0, concat_axis=0, tiled=True)
    q_rows = replies.reshape(table_slots, width)[target]
    rem_rows = lax.optimization_barrier(remainder_table[flat_r].astype(jnp.bfloat16))
    cot_wide = cot_rows.astype(jnp.float32)
    q_terms = (cot_wide * rem_rows.astype(jnp.float32)).astype(jnp.bfloat16)
    r_values = (cot_wide * q_rows.astype(jnp.float32)).astype(jnp.bfloat16)
    outgoing = (
        jnp.zeros((table_slots, width), jnp.bfloat16)
        .at[target]
        .set(q_terms)
        .reshape(devices, capacity, width)
    )
    arrived = lax.all_to_all(outgoing, ("gx", "gy"), split_axis=0, concat_axis=0, tiled=True)
    q_values = arrived.reshape(table_slots, width)
    quotient_grad = block_sums(asked_flat, q_values, q_dev)
    new_quotient, new_quotient_acc = adagrad(quotient_table, quotient_acc, quotient_grad)
    first = lax.axis_index(("gx", "gy")) * share
    partial_grad = block_sums(flat_r, r_values, r_rows)
    total = lax.psum(partial_grad, ("gx", "gy"))
    grad_share = lax.dynamic_slice_in_dim(total, first, share, 0)
    param_share = lax.dynamic_slice_in_dim(remainder_table, first, share, 0)
    new_share, new_remainder_acc = adagrad(param_share, remainder_acc, grad_share)
    new_remainder = lax.all_gather(new_share, ("gx", "gy"), axis=0, tiled=True)
    return (new_quotient, new_quotient_acc, new_remainder, new_remainder_acc)


def solution(mesh):
    return jax.shard_map(
        local,
        mesh=mesh,
        in_specs=(
            P(("gx", "gy"), None),
            P(("gx", "gy"), None),
            P(),
            P(("gx", "gy"), None),
            P(("gx", "gy"), None),
            P(("gx", "gy"), None),
            P(("gx", "gy"), None),
        ),
        out_specs=(P(("gx", "gy"), None), P(("gx", "gy"), None), P(), P(("gx", "gy"), None)),
        check_vma=False,
    )
```

profile of v0, /device:TPU:0, one launch (start us, length us, event | category | flops | bytes accessed | tf_op | source)
XLA Modules:
  0.0 350.6 jit_solution(3329541990858526170)
XLA Ops:
  7.2 0.8 copy.16
  8.0 0.1 reshape.172
  8.1 0.1 convert_reduce_fusion
  8.4 0.1 reduce.1
  8.5 0.7 fusion.24
  9.2 0.7 fusion.23
  9.9 5.0 %sort.17 = (s32[1280]{0:T(1024)}, s32[1280]{0:T(1024)S(1)}) sort(s32[1280]{0:T(1024)S(1)} %get-tuple-element.98, s32[1280]{0:T(1024)S(1)} %iota.24), dimensions={0}, to_apply=%region_0.1 | sort | flops 14080 | bytes 20480 | tf_op jit(solution)/shard_map/jit(argsort)/sort | solution.py:50
  15.0 7.1 %gather_fusion = s32[1280]{0:T(1024)S(1)} fusion(s32[1280]{0:T(1024)S(1)} %get-tuple-element.98, s32[2048]{0:T(1024)S(1)} %pad_clamp_fusion.3), kind=kCustom, calls=%fused_computation | custom fusion | bytes 15360 | tf_op jit(solution)/shard_map/gather | solution.py:51
  22.1 4.3 %fusion.19 = (s32[1280]{0:T(1024)S(1)}, s32[1280,1]{0,1:T(1,128)S(1)}) fusion(s32[]{:T(128)} %bitcast.28, s32[]{:T(128)} %bitcast.29, s32[]{:T(128)} %bitcast.30, s32[]{:T(128)} %bitcast.31, s32[]{:T(128)} %bitcast.32, s32[]{:T(128)} %bitcast.34, s32[]{:T(128)} %bitcast.33, s32[1280]{0:T(1024)S(1)} %gather_fusion), kind=kLoop, calls=%fused_computation.79 | loop fusion | flops 19200 | bytes 15388 | tf_op jit(solution)/shard_map/gather | solution.py:55
  26.4 0.4 compare_reduce_fusion.24
  26.8 15.8 %select_subtract_fusion = s32[1280]{0:T(1024)S(1)} fusion(pred[1280]{0:T(1024)(128)(4,1)S(1)} %get-tuple-element.80, pred[1280]{0:T(1024)(128)(4,1)S(1)} %get-tuple-element.79, pred[1280]{0:T(1024)(128)(4,1)S(1)} %get-tuple-element.78, pred[1280]{0:T(1024)(128)(4,1)S(1)} %get-tuple-element.77, pred[1280]{0:T(1024)(128)(4,1)S(1)} %get-tuple-element.76, ...), kind=kLoop, calls=%fused_computation.73 | loop fusion | flops 35840 | bytes 47460 | tf_op jit(solution)/shard_map/sub | solution.py:55
  42.6 5.2 %scatter_custom_fusion = s32[1280]{0:T(1024)S(1)} fusion(s32[1280]{0:T(1024)S(1)} %compare_select_fusion.4, s32[1280]{0:T(1024)S(1)} %select_subtract_fusion, s32[]{:T(128)} %constant.26.clone.1), kind=kCustom, calls=%fused_computation.81 | custom fusion | bytes 5124 | tf_op jit(solution)/shard_map/scatter | solution.py:56
  47.8 5.3 %scatter_custom_fusion.1 = s32[2560]{0:T(1024)S(1)} fusion(s32[1280]{0:T(1024)S(1)} %compare_select_fusion.3, s32[1280]{0:T(1024)S(1)} %get-tuple-element.97, s32[]{:T(128)} %constant.26.clone.1), kind=kCustom, calls=%fused_computation.77 | custom fusion | bytes 10244 | tf_op jit(solution)/shard_map/scatter | solution.py:58
  53.1 0.1 all_to_all.12
  53.2 14.3 %all_to_all.19 = s32[32,1,80]{2,1,0:T(1,128)S(1)} all-to-all(s32[32,1,80]{2,1,0:T(1,128)S(1)} %all_to_all.12), channel_id=1, replica_groups=mesh['gx'=8,'gy'=4] {'gx','gy'}, dimensions={0} | all-to-all | bytes 20480 | tf_op jit(solution)/shard_map/all_to_all | solution.py:61
  67.7 6.8 %gather_fusion.2 = bf16[2560,256]{1,0:T(8,128)(2,1)} fusion(f32[1024,256]{1,0:T(8,128)S(1)} %copy-done, s32[3072]{0:T(1024)S(1)} %pad_clamp_fusion), kind=kCustom, calls=%fused_computation.2 | custom fusion | bytes 2631680 | tf_op jit(solution)/shard_map/gather | solution.py:63
  74.5 2.8 all-to-all-start.2
  77.3 1.3 broadcast_in_dim.37
  78.6 2.5 convert_element_type.37
  81.1 0.1 eq.100
  81.3 26.4 %all-to-all-done.2 = bf16[32,80,256]{2,1,0:T(8,128)(2,1)S(1)} async-done(((bf16[32,80,256]{2,1,0:T(8,128)(2,1)}), bf16[32,80,256]{2,1,0:T(8,128)(2,1)S(1)}, u32[]{:S(2)}, u32[]{:S(2)}) %all-to-all-start.2) | async-done | bytes 1310752 | tf_op jit(solution)/shard_map/all_to_all | solution.py:64
  107.6 4.1 %gather_fusion.3 = bf16[1280,256]{1,0:T(8,128)(2,1)S(1)} fusion(bf16[2560,256]{1,0:T(8,128)(2,1)S(1)} %bitcast.55, s32[2048]{0:T(1024)S(1)} %pad_clamp_fusion.1), kind=kCustom, calls=%fused_computation.3 | custom fusion | bytes 1315840 | tf_op jit(solution)/shard_map/gather | solution.py:65
  111.7 1.5 multiply_convert_fusion
  113.2 12.5 %while.3 = (s32[]{:T(128)}, f32[4,1024,256]{2,1,0:T(8,128)}, s32[4]{0:T(128)S(1)}, s32[64,20]{1,0:T(8,128)}, bf16[1280,256]{1,0:T(8,128)(2,1)S(1)}, /*index=5*/s32[1280]{0:T(1024)S(1)}, s32[]{:T(128)}) while((s32[]{:T(128)}, f32[4,1024,256]{2,1,0:T(8,128)}, s32[4]{0:T(128)S(1)}, s32[64,20]{1,0:T(8,128)}, ...), condition=%wide.wide.region_7.8_spmd, body=%wide.wide.region_6.7_spmd.sunk | while | flops 672400384 | bytes 1717853 | solution.py:26
  113.2 0.6 dynamic_slice.21
  113.8 0.6 iota_add_fusion.3
  114.4 1.9 fusion.35
  116.3 0.6 dynamic_slice.21
  116.9 0.6 iota_add_fusion.3
  117.5 1.9 fusion.35
  119.4 0.6 dynamic_slice.21
  120.0 0.6 iota_add_fusion.3
  120.7 1.9 fusion.35
  122.6 0.6 dynamic_slice.21
  123.1 0.6 iota_add_fusion.3
  123.8 1.9 fusion.35
  125.8 142.5 %all-reduce.2.cloned.1.call-done = f32[4096,256]{1,0:T(8,128)} async-done(((f32[4096,256]{1,0:T(8,128)}), f32[4096,256]{1,0:T(8,128)}) %all-reduce.2.cloned.1.call-update) | async-done | bytes 4194320 | tf_op jit(solution)/shard_map/psum | solution.py:82
  268.3 1.7 divide_subtract_fusion.1
  270.0 0.1 reshape.175
  270.2 5.4 %gather_fusion.1 = bf16[1280,256]{1,0:T(8,128)(2,1)S(1)} fusion(f32[4096,256]{1,0:T(8,128)} %param.11, s32[2048]{0:T(1024)S(1)} %pad_clamp_fusion.2), kind=kCustom, calls=%fused_computation.1 | custom fusion | bytes 1315840 | tf_op jit(solution)/shard_map/gather | solution.py:66
  275.6 9.3 %scatter_custom_fusion.2 = bf16[2560,256]{1,0:T(8,128)(2,1)} fusion(s32[1280]{0:T(1024)S(1)} %compare_select_fusion.3, f32[1280,256]{1,0:T(8,128)S(1)} %copy-done.1, bf16[1280,256]{1,0:T(8,128)(2,1)S(1)} %gather_fusion.1, bf16[]{:T(256)} %constant.39.clone.1), kind=kCustom, calls=%fused_computation.21 | custom fusion | flops 983040 | bytes 3276802 | tf_op jit(solution)/shard_map/scatter | solution.py:73
  284.9 3.9 %all-to-all-start.1 = ((bf16[32,80,256]{2,1,0:T(8,128)(2,1)}), bf16[32,80,256]{2,1,0:T(8,128)(2,1)S(1)}, u32[]{:S(2)}, u32[]{:S(2)}) async-start(bf16[32,80,256]{2,1,0:T(8,128)(2,1)} %bitcast.57), calls=%async_computation.1 | async-start | bytes 2621440 | tf_op jit(solution)/shard_map/all_to_all | solution.py:76
  288.8 0.5 broadcast.375
  289.3 0.7 reduce.62
  290.1 39.1 %all-to-all-done.1 = bf16[32,80,256]{2,1,0:T(8,128)(2,1)S(1)} async-done(((bf16[32,80,256]{2,1,0:T(8,128)(2,1)}), bf16[32,80,256]{2,1,0:T(8,128)(2,1)S(1)}, u32[]{:S(2)}, u32[]{:S(2)}) %all-to-all-start.1) | async-done | bytes 1310752 | tf_op jit(solution)/shard_map/all_to_all | solution.py:76
  329.1 4.7 %divide_subtract_fusion = (f32[1024,256]{1,0:T(8,128)}, f32[1024,256]{1,0:T(8,128)}) fusion(f32[1024,256]{1,0:T(8,128)S(1)} %copy-done, f32[1024,256]{1,0:T(8,128)} %param.10, bf16[2560,256]{1,0:T(8,128)(2,1)S(1)} %bitcast.59, s32[2560]{0:T(1024)S(1)} %eq.54), kind=kOutput, calls=%fused_computation.19 | convolution fusion | flops 1346371584 | bytes 5515264 | tf_op jit(solution)/shard_map/while/body/eval_jaxpr/dot_general | solution.py:23
  333.8 5.5 %all-gather.2.cloned.1.call-done = f32[4096,256]{1,0:T(8,128)} async-done(((f32[128,256]{1,0:T(8,128)}), f32[4096,256]{1,0:T(8,128)}) %all-gather.2.cloned.1.call-update) | async-done | bytes 4194320 | tf_op jit(solution)/shard_map/all_gather | solution.py:86
  339.3 4.5 %copy.29 = f32[4096,256]{1,0:T(8,128)} copy(f32[4096,256]{1,0:T(8,128)} %all-gather.2.cloned.1.call-done) | data formatting | bytes 8388608
  (36 shorter events, 0.7 us)
Async XLA Ops:
  15.0 52.7 %copy-start = (f32[1024,256]{1,0:T(8,128)S(1)}, f32[1024,256]{1,0:T(8,128)}, u32[]{:S(2)}) copy-start(f32[1024,256]{1,0:T(8,128)} %param.9) | copy-start | bytes 3145732
  74.5 2.9 copy-start.5
  74.5 33.2 %all-to-all-start.2 = ((bf16[32,80,256]{2,1,0:T(8,128)(2,1)}), bf16[32,80,256]{2,1,0:T(8,128)(2,1)S(1)}, u32[]{:S(2)}, u32[]{:S(2)}) async-start(bf16[32,80,256]{2,1,0:T(8,128)(2,1)} %bitcast.56), calls=%async_computation.2 | async-start | bytes 2621440 | tf_op jit(solution)/shard_map/all_to_all | solution.py:64
  77.3 191.0 %all-reduce.2.cloned.1.call-start = ((), (), s32[]{:S(2)}) async-start(), calls=%async_computation.3 | async-start | bytes 8388608 | tf_op jit(solution)/shard_map/psum | solution.py:82
  78.6 2.5 copy-start.6
  81.1 30.6 %copy-start.2 = (s32[64,20]{1,0:T(8,128)}, s32[64,20]{1,0:T(8,128)S(1)}, u32[]{:S(2)}) copy-start(s32[64,20]{1,0:T(8,128)S(1)} %copy.18) | copy-start | bytes 15364
  125.7 142.6 %copy-start.4 = (f32[128,256]{1,0:T(8,128)S(1)}, f32[128,256]{1,0:T(8,128)}, u32[]{:S(2)}) copy-start(f32[128,256]{1,0:T(8,128)} %param.12) | copy-start | bytes 393220
  125.7 144.3 %copy-start.3 = (s32[64,20]{1,0:T(8,128)S(1)}, s32[64,20]{1,0:T(8,128)}, u32[]{:S(2)}) copy-start(s32[64,20]{1,0:T(8,128)} %get-tuple-element.230) | copy-start | bytes 15364
  125.7 213.6 %all-gather.2.cloned.1.call-start = ((), (), s32[]{:S(2)}) async-start(), calls=%async_computation.4 | async-start | bytes 4325376 | tf_op jit(solution)/shard_map/all_gather | solution.py:86
  270.2 5.4 %copy-start.1 = (f32[1280,256]{1,0:T(8,128)S(1)}, f32[1280,256]{1,0:T(8,128)}, u32[]{:S(2)}) copy-start(f32[1280,256]{1,0:T(8,128)} %convert_element_type.37) | copy-start | bytes 3932164
  284.9 44.2 %all-to-all-start.1 = ((bf16[32,80,256]{2,1,0:T(8,128)(2,1)}), bf16[32,80,256]{2,1,0:T(8,128)(2,1)S(1)}, u32[]{:S(2)}, u32[]{:S(2)}) async-start(bf16[32,80,256]{2,1,0:T(8,128)(2,1)} %bitcast.57), calls=%async_computation.1 | async-start | bytes 2621440 | tf_op jit(solution)/shard_map/all_to_all | solution.py:76
Sparse Core Ops, SparseCore 0:
  125.8 142.3 all-reduce.1
  271.3 68.0 all-gather.1
where the time goes:
time: 352 us; the launch traced here: 351 us
  waiting for transfers between devices  213 us (61%)
  local copies, waits for them, and re-layouts  47.9 us (14%)
  other arithmetic  41.6 us (12%)
  blocking collectives  14.3 us (4%)
  between operations  14.3 us (4%)
  matrix products  12.2 us (3%)
  starting transfers between devices  6.77 us (2%)
    psum x1, waiting for transfers between devices, local(): total = lax.psum(partial_grad, ('gx', 'gy'))  142 us
    all_to_all x1, waiting for transfers between devices, local(): lax.all_to_all(outgoing, ('gx', 'gy'), split_axis=0, concat_axis=0, tiled...  39.1 us
    all_to_all x1, waiting for transfers between devices, local(): lax.all_to_all(found, ('gx', 'gy'), split_axis=0, concat_axis=0, tiled=True)  26.4 us
    sub x1, other arithmetic, local(): sorted_owner * capacity + jnp.arange(count, dtype=jnp.int32)  15.8 us
    all_to_all x1, blocking collectives, local(): lax.all_to_all(local_sent, ('gx', 'gy'), split_axis=0, concat_axis=0, til...  14.3 us
    dot_general x5, matrix products, one(): return jnp.dot(hit, values, preferred_element_type=jnp.float32)  12.2 us
    scatter x1, other arithmetic, local(): outgoing = jnp.zeros((table_slots, width), jnp.bfloat16).at[target].set(q...  9.26 us
    gather x1, local copies, waits for them, and re-layouts, local(): sorted_owner = owner[order]  7.08 us
  transfers between devices with their start and end apart: 4, of which 4 were waited for; matrix products, arithmetic and copies ran while one was open for 7% of the time, Pallas kernels for 0%

commit v1 on v0

--- a/solution.py
+++ b/solution.py
@@ -79,7 +79,11 @@
     new_quotient, new_quotient_acc = adagrad(quotient_table, quotient_acc, quotient_grad)
     first = lax.axis_index(("gx", "gy")) * share
     partial_grad = block_sums(flat_r, r_values, r_rows)
-    total = lax.psum(partial_grad, ("gx", "gy"))
+
+    def supply_core_over_axis(page):
+        return lax.psum(lax.psum(page, axis_name="gy"), axis_name="gx")
+
+    total = supply_core_over_axis(partial_grad)
     grad_share = lax.dynamic_slice_in_dim(total, first, share, 0)
     param_share = lax.dynamic_slice_in_dim(remainder_table, first, share, 0)
     new_share, new_remainder_acc = adagrad(param_share, remainder_acc, grad_share)

time: 352 us -> 448 us (1.27)
  waiting for transfers between devices: 213 us -> 309 us
    psum x1 -> x2, waiting for transfers between devices: 142 us -> 238 us  [supply_core_over_axis(): return lax.psum(lax.psum(page, axis_name='gy'), axis_name='gx')]
  transfers between devices with their start and end apart: 4 -> 5, of which waited for: 4 -> 5; matrix products, arithmetic and copies ran while one was open for 7% -> 6% of each run, Pallas kernels for 0% -> 0%
where the time goes in v1:
time: 448 us; the launch traced here: 447 us
  waiting for transfers between devices  309 us (69%)
  local copies, waits for them, and re-layouts  48 us (11%)
  other arithmetic  41.6 us (9%)
  blocking collectives  14.3 us (3%)
  between operations  14 us (3%)
  matrix products  12.2 us (3%)
  starting transfers between devices  7.58 us (2%)
    psum x2, waiting for transfers between devices, supply_core_over_axis(): return lax.psum(lax.psum(page, axis_name='gy'), axis_name='gx')  238 us
    all_to_all x1, waiting for transfers between devices, local(): lax.all_to_all(outgoing, ('gx', 'gy'), split_axis=0, concat_axis=0, tiled...  39 us
    all_to_all x1, waiting for transfers between devices, local(): lax.all_to_all(found, ('gx', 'gy'), split_axis=0, concat_axis=0, tiled=True)  26.3 us
    sub x1, other arithmetic, local(): sorted_owner * capacity + jnp.arange(count, dtype=jnp.int32)  15.8 us
    all_to_all x1, blocking collectives, local(): lax.all_to_all(local_sent, ('gx', 'gy'), split_axis=0, concat_axis=0, til...  14.3 us
    dot_general x5, matrix products, one(): return jnp.dot(hit, values, preferred_element_type=jnp.float32)  12.2 us
    scatter x1, other arithmetic, local(): outgoing = jnp.zeros((table_slots, width), jnp.bfloat16).at[target].set(q...  9.26 us
  transfers between devices with their start and end apart: 5, of which 5 were waited for; matrix products, arithmetic and copies ran while one was open for 6% of the time, Pallas kernels for 0%

profile of v1, /device:TPU:0, one launch (start us, length us, event | category | flops | bytes accessed | tf_op | source)
XLA Modules:
  0.0 446.8 jit_solution(3900428368517834728)
XLA Ops:
  7.2 0.8 copy.16
  8.0 0.1 reshape.172
  8.1 0.1 convert_reduce_fusion
  8.4 0.1 reduce.1
  8.5 0.7 fusion.24
  9.2 0.7 fusion.23
  9.9 5.0 %sort.17 = (s32[1280]{0:T(1024)}, s32[1280]{0:T(1024)S(1)}) sort(s32[1280]{0:T(1024)S(1)} %get-tuple-element.98, s32[1280]{0:T(1024)S(1)} %iota.24), dimensions={0}, to_apply=%region_0.1 | sort | flops 14080 | bytes 20480 | tf_op jit(solution)/shard_map/jit(argsort)/sort | solution.py:50
  15.0 7.1 %gather_fusion = s32[1280]{0:T(1024)S(1)} fusion(s32[1280]{0:T(1024)S(1)} %get-tuple-element.98, s32[2048]{0:T(1024)S(1)} %pad_clamp_fusion.3), kind=kCustom, calls=%fused_computation | custom fusion | bytes 15360 | tf_op jit(solution)/shard_map/gather | solution.py:51
  22.1 4.3 fusion.19
  26.4 0.4 compare_reduce_fusion.24
  26.8 15.8 %select_subtract_fusion = s32[1280]{0:T(1024)S(1)} fusion(pred[1280]{0:T(1024)(128)(4,1)S(1)} %get-tuple-element.80, pred[1280]{0:T(1024)(128)(4,1)S(1)} %get-tuple-element.79, pred[1280]{0:T(1024)(128)(4,1)S(1)} %get-tuple-element.78, pred[1280]{0:T(1024)(128)(4,1)S(1)} %get-tuple-element.77, pred[1280]{0:T(1024)(128)(4,1)S(1)} %get-tuple-element.76, ...), kind=kLoop, calls=%fused_computation.73 | loop fusion | flops 35840 | bytes 47460 | tf_op jit(solution)/shard_map/sub | solution.py:55
  42.6 5.2 %scatter_custom_fusion = s32[1280]{0:T(1024)S(1)} fusion(s32[1280]{0:T(1024)S(1)} %compare_select_fusion.4, s32[1280]{0:T(1024)S(1)} %select_subtract_fusion, s32[]{:T(128)} %constant.26.clone.1), kind=kCustom, calls=%fused_computation.81 | custom fusion | bytes 5124 | tf_op jit(solution)/shard_map/scatter | solution.py:56
  47.8 5.3 %scatter_custom_fusion.1 = s32[2560]{0:T(1024)S(1)} fusion(s32[1280]{0:T(1024)S(1)} %compare_select_fusion.3, s32[1280]{0:T(1024)S(1)} %get-tuple-element.97, s32[]{:T(128)} %constant.26.clone.1), kind=kCustom, calls=%fused_computation.77 | custom fusion | bytes 10244 | tf_op jit(solution)/shard_map/scatter | solution.py:58
  53.2 14.3 %all_to_all.19 = s32[32,1,80]{2,1,0:T(1,128)S(1)} all-to-all(s32[32,1,80]{2,1,0:T(1,128)S(1)} %all_to_all.12), channel_id=1, replica_groups=mesh['gx'=8,'gy'=4] {'gx','gy'}, dimensions={0} | all-to-all | bytes 20480 | tf_op jit(solution)/shard_map/all_to_all | solution.py:61
  67.7 6.8 %gather_fusion.2 = bf16[2560,256]{1,0:T(8,128)(2,1)} fusion(f32[1024,256]{1,0:T(8,128)S(1)} %copy-done, s32[3072]{0:T(1024)S(1)} %pad_clamp_fusion), kind=kCustom, calls=%fused_computation.2 | custom fusion | bytes 2631680 | tf_op jit(solution)/shard_map/gather | solution.py:63
  74.5 2.8 all-to-all-start.2
  77.3 1.3 broadcast_in_dim.37
  78.6 2.6 convert_element_type.37
  81.2 0.1 eq.100
  81.4 26.3 %all-to-all-done.2 = bf16[32,80,256]{2,1,0:T(8,128)(2,1)S(1)} async-done(((bf16[32,80,256]{2,1,0:T(8,128)(2,1)}), bf16[32,80,256]{2,1,0:T(8,128)(2,1)S(1)}, u32[]{:S(2)}, u32[]{:S(2)}) %all-to-all-start.2) | async-done | bytes 1310752 | tf_op jit(solution)/shard_map/all_to_all | solution.py:64
  107.6 4.1 gather_fusion.3
  111.7 1.5 multiply_convert_fusion
  113.2 12.5 %while.3 = (s32[]{:T(128)}, f32[4,1024,256]{2,1,0:T(8,128)}, s32[4]{0:T(128)S(1)}, s32[64,20]{1,0:T(8,128)}, bf16[1280,256]{1,0:T(8,128)(2,1)S(1)}, /*index=5*/s32[1280]{0:T(1024)S(1)}, s32[]{:T(128)}) while((s32[]{:T(128)}, f32[4,1024,256]{2,1,0:T(8,128)}, s32[4]{0:T(128)S(1)}, s32[64,20]{1,0:T(8,128)}, ...), condition=%wide.wide.region_7.8_spmd, body=%wide.wide.region_6.7_spmd.sunk | while | flops 672400384 | bytes 1717853 | solution.py:26
  113.2 0.6 dynamic_slice.21
  113.8 0.6 iota_add_fusion.3
  114.4 1.9 fusion.35
  116.3 0.6 dynamic_slice.21
  116.9 0.6 iota_add_fusion.3
  117.5 1.9 fusion.35
  119.4 0.6 dynamic_slice.21
  120.0 0.6 iota_add_fusion.3
  120.7 1.9 fusion.35
  122.6 0.6 dynamic_slice.21
  123.1 0.6 iota_add_fusion.3
  123.8 1.9 fusion.35
  125.8 155.1 %all-reduce.3.cloned.1.call-done = f32[4096,256]{1,0:T(8,128)} async-done(((f32[4096,256]{1,0:T(8,128)}), f32[4096,256]{1,0:T(8,128)}) %all-reduce.3.cloned.1.call-update) | async-done | bytes 4194320 | tf_op jit(solution)/shard_map/psum | solution.py:84
  280.9 83.0 %all-reduce.5.cloned.1.call-done = f32[4096,256]{1,0:T(8,128)} async-done(((f32[4096,256]{1,0:T(8,128)}), f32[4096,256]{1,0:T(8,128)}) %all-reduce.5.cloned.1.call-update) | async-done | bytes 4194320 | tf_op jit(solution)/shard_map/psum | solution.py:84
  364.0 1.7 divide_subtract_fusion.1
  365.7 0.1 reshape.175
  365.9 5.4 %gather_fusion.1 = bf16[1280,256]{1,0:T(8,128)(2,1)S(1)} fusion(f32[4096,256]{1,0:T(8,128)} %param.11, s32[2048]{0:T(1024)S(1)} %pad_clamp_fusion.2), kind=kCustom, calls=%fused_computation.1 | custom fusion | bytes 1315840 | tf_op jit(solution)/shard_map/gather | solution.py:66
  371.3 9.3 %scatter_custom_fusion.2 = bf16[2560,256]{1,0:T(8,128)(2,1)} fusion(s32[1280]{0:T(1024)S(1)} %compare_select_fusion.3, f32[1280,256]{1,0:T(8,128)S(1)} %copy-done.1, bf16[1280,256]{1,0:T(8,128)(2,1)S(1)} %gather_fusion.1, bf16[]{:T(256)} %constant.39.clone.1), kind=kCustom, calls=%fused_computation.21 | custom fusion | flops 983040 | bytes 3276802 | tf_op jit(solution)/shard_map/scatter | solution.py:73
  380.6 4.7 %all-to-all-start.1 = ((bf16[32,80,256]{2,1,0:T(8,128)(2,1)}), bf16[32,80,256]{2,1,0:T(8,128)(2,1)S(1)}, u32[]{:S(2)}, u32[]{:S(2)}) async-start(bf16[32,80,256]{2,1,0:T(8,128)(2,1)} %bitcast.57), calls=%async_computation.1 | async-start | bytes 2621440 | tf_op jit(solution)/shard_map/all_to_all | solution.py:76
  385.2 0.5 broadcast.375
  385.8 0.7 reduce.62
  386.5 39.0 %all-to-all-done.1 = bf16[32,80,256]{2,1,0:T(8,128)(2,1)S(1)} async-done(((bf16[32,80,256]{2,1,0:T(8,128)(2,1)}), bf16[32,80,256]{2,1,0:T(8,128)(2,1)S(1)}, u32[]{:S(2)}, u32[]{:S(2)}) %all-to-all-start.1) | async-done | bytes 1310752 | tf_op jit(solution)/shard_map/all_to_all | solution.py:76
  425.5 4.7 %divide_subtract_fusion = (f32[1024,256]{1,0:T(8,128)}, f32[1024,256]{1,0:T(8,128)}) fusion(f32[1024,256]{1,0:T(8,128)S(1)} %copy-done, f32[1024,256]{1,0:T(8,128)} %param.10, bf16[2560,256]{1,0:T(8,128)(2,1)S(1)} %bitcast.59, s32[2560]{0:T(1024)S(1)} %eq.54), kind=kOutput, calls=%fused_computation.19 | convolution fusion | flops 1346371584 | bytes 5515264 | tf_op jit(solution)/shard_map/while/body/eval_jaxpr/dot_general | solution.py:23
  430.2 5.6 %all-gather.2.cloned.1.call-done = f32[4096,256]{1,0:T(8,128)} async-done(((f32[128,256]{1,0:T(8,128)}), f32[4096,256]{1,0:T(8,128)}) %all-gather.2.cloned.1.call-update) | async-done | bytes 4194320 | tf_op jit(solution)/shard_map/all_gather | solution.py:90
  435.8 4.5 %copy.30 = f32[4096,256]{1,0:T(8,128)} copy(f32[4096,256]{1,0:T(8,128)} %all-gather.2.cloned.1.call-done) | data formatting | bytes 8388608
  (39 shorter events, 0.8 us)
Async XLA Ops:
  15.0 52.7 %copy-start = (f32[1024,256]{1,0:T(8,128)S(1)}, f32[1024,256]{1,0:T(8,128)}, u32[]{:S(2)}) copy-start(f32[1024,256]{1,0:T(8,128)} %param.9) | copy-start | bytes 3145732
  74.5 2.9 copy-start.5
  74.5 33.2 %all-to-all-start.2 = ((bf16[32,80,256]{2,1,0:T(8,128)(2,1)}), bf16[32,80,256]{2,1,0:T(8,128)(2,1)S(1)}, u32[]{:S(2)}, u32[]{:S(2)}) async-start(bf16[32,80,256]{2,1,0:T(8,128)(2,1)} %bitcast.56), calls=%async_computation.2 | async-start | bytes 2621440 | tf_op jit(solution)/shard_map/all_to_all | solution.py:64
  77.3 203.6 %all-reduce.3.cloned.1.call-start = ((), (), s32[]{:S(2)}) async-start(), calls=%async_computation.3 | async-start | bytes 8388608 | tf_op jit(solution)/shard_map/psum | solution.py:84
  78.6 2.6 copy-start.6
  81.2 30.4 %copy-start.2 = (s32[64,20]{1,0:T(8,128)}, s32[64,20]{1,0:T(8,128)S(1)}, u32[]{:S(2)}) copy-start(s32[64,20]{1,0:T(8,128)S(1)} %copy.18) | copy-start | bytes 15364
  125.7 238.2 %all-reduce.5.cloned.1.call-start = ((), (), s32[]{:S(2)}) async-start(), calls=%async_computation.4 | async-start | bytes 8388608 | tf_op jit(solution)/shard_map/psum | solution.py:84
  280.9 83.1 %copy-start.4 = (f32[128,256]{1,0:T(8,128)S(1)}, f32[128,256]{1,0:T(8,128)}, u32[]{:S(2)}) copy-start(f32[128,256]{1,0:T(8,128)} %param.12) | copy-start | bytes 393220
  280.9 84.8 %copy-start.3 = (s32[64,20]{1,0:T(8,128)S(1)}, s32[64,20]{1,0:T(8,128)}, u32[]{:S(2)}) copy-start(s32[64,20]{1,0:T(8,128)} %get-tuple-element.234) | copy-start | bytes 15364
  280.9 154.9 %all-gather.2.cloned.1.call-start = ((), (), s32[]{:S(2)}) async-start(), calls=%async_computation.5 | async-start | bytes 4325376 | tf_op jit(solution)/shard_map/all_gather | solution.py:90
  365.9 5.4 %copy-start.1 = (f32[1280,256]{1,0:T(8,128)S(1)}, f32[1280,256]{1,0:T(8,128)}, u32[]{:S(2)}) copy-start(f32[1280,256]{1,0:T(8,128)} %convert_element_type.37) | copy-start | bytes 3932164
  380.6 45.0 %all-to-all-start.1 = ((bf16[32,80,256]{2,1,0:T(8,128)(2,1)}), bf16[32,80,256]{2,1,0:T(8,128)(2,1)S(1)}, u32[]{:S(2)}, u32[]{:S(2)}) async-start(bf16[32,80,256]{2,1,0:T(8,128)(2,1)} %bitcast.57), calls=%async_computation.1 | async-start | bytes 2621440 | tf_op jit(solution)/shard_map/all_to_all | solution.py:76
Sparse Core Ops, SparseCore 0:
  125.8 154.9 all-reduce.2
  284.1 79.7 all-reduce.4
  367.0 68.8 all-gather.1
